TPU v7x, 256 devices: a whole 4x4x8 slice. The times are simulated.
256 devices in a mesh: slab: 64 (over x, z, core), img: 4 (over y).
Axes of the slice: x: 4, y: 4, z: 8, core: 2. Of those that a mesh axis runs over, the one named last changes fastest.
Arguments:
- volume: bfloat16 [32768, 256], P('slab'), may hold values from -6 to 6
- interp: bfloat16 [4, 64, 16, 32768], P('img', None, None, 'slab'), may hold values from -0.09375 to 0.09375
- block_index: int32 [4, 64, 64], P('img'), may hold values from 0 to 7
- images: bfloat16 [4, 1024, 128, 256], P('img', 'slab'), may hold values from -6 to 6
- defocus: float32 [4, 1024], P('img', 'slab'), may hold values from 5000 to 25000
- orient: int32 [4, 1024, 4], P('img', 'slab'), may hold values from 0 to 63, all different within a row
Outputs:
- update: float32 [32768, 256], P('slab')
- weights: float32 [4, 1024, 64], P('img', 'slab')
Inputs may be any that keep to these rules, and one draw needn't show every extreme that they name: `orient`: each image lists 4 different orientations of its group.
All inputs are finite; a program needn't handle non-finite values.
Results may differ from a plain program's by a relative error of at most 0.0077.
Values may be sent and summed in bfloat16 or wider, within the bound.
A program may use at most 64 MiB of HBM per device.

v0:
```python
import math
import jax
import jax.numpy as jnp
from jax import lax
from jax.sharding import PartitionSpec as P

BOX = 256
NS = 16
wave_length = 0.0197
aberration = 27000000.0
amplitude = 0.1
grid_side = 4


def phase_tables(fourier, shifts, box):
    freq = (jnp.arange(fourier, dtype=jnp.int32) - fourier // 2).astype(jnp.float32)
    shift_steps = jnp.arange(shifts, dtype=jnp.int32)
    shift_x = (2 * (shift_steps // grid_side) - (grid_side - 1)).astype(jnp.float32)
    shift_y = (2 * (shift_steps % grid_side) - (grid_side - 1)).astype(jnp.float32)
    angle = 2.0 * math.pi / box * (freq[:, None, None] * shift_x + freq[None, :, None] * shift_y)
    forward = jnp.stack([jnp.cos(angle), jnp.sin(angle)], axis=1).reshape(
        2 * fourier * fourier, shifts
    )
    backward = jnp.stack([jnp.cos(angle), -jnp.sin(angle)], axis=1).reshape(
        2 * fourier * fourier, shifts
    )
    return (forward.astype(jnp.bfloat16), backward.T.astype(jnp.bfloat16))


def contrast(defocus_blk, fourier, box):
    freq = (jnp.arange(fourier, dtype=jnp.int32) - fourier // 2).astype(jnp.float32)
    wave_sq = (freq[:, None] * freq[:, None] + freq[None, :] * freq[None, :]) / (box * box)
    phase = math.pi * wave_length * defocus_blk[:, None, None] * wave_sq
    phase = phase - 0.5 * math.pi * aberration * wave_length**3 * wave_sq * wave_sq
    return -(math.sqrt(1.0 - amplitude * amplitude) * jnp.sin(phase) + amplitude * jnp.cos(phase))


def correlate(panels, image_blk, list_blk, defocus_blk, phase_fwd, phase_back, box):
    count = image_blk.shape[0]
    fourier = image_blk.shape[1]
    picks = list_blk.shape[1]
    shifts = phase_fwd.shape[1]
    ctf = contrast(defocus_blk, fourier, box)
    weighted = ctf[:, :, None, :] * image_blk.astype(jnp.float32).reshape(
        count, fourier, 2, fourier
    )
    real_u = weighted[:, None, :, 0]
    imag_u = weighted[:, None, :, 1]
    chosen = panels[list_blk].astype(jnp.float32).reshape(count, picks, fourier, 2, fourier)
    real_p = chosen[:, :, :, 0]
    imag_p = chosen[:, :, :, 1]
    product = jnp.stack(
        [real_p * real_u + imag_p * imag_u, real_p * imag_u - imag_p * real_u], axis=3
    )
    product = product.astype(jnp.bfloat16).reshape(count * picks, 2 * fourier * fourier)
    scores = jnp.dot(product, phase_fwd, preferred_element_type=jnp.float32) / fourier
    scores = scores.reshape(count, picks * shifts)
    squared = scores * scores
    weights = squared / (jnp.mean(squared, axis=1, keepdims=True) + 1e-05)
    rounded = weights.astype(jnp.bfloat16).reshape(count * picks, shifts)
    spread = jnp.dot(rounded, phase_back, preferred_element_type=jnp.float32)
    spread = spread.reshape(count, picks, fourier, 2, fourier)
    real_e = spread[:, :, :, 0]
    imag_e = spread[:, :, :, 1]
    backed = jnp.stack(
        [real_u * real_e - imag_u * imag_e, real_u * imag_e + imag_u * real_e], axis=3
    )
    backed = backed.astype(jnp.bfloat16).reshape(count * picks, 2 * fourier * fourier)
    return (weights, backed)


def on_device(volume, interp, block_index, images, defocus, orient):
    slab_count = lax.axis_size("slab")
    slab_index = lax.axis_index("slab")
    orient_count = interp.shape[1]
    ori_dev = orient_count // slab_count
    block_rows = interp.shape[2]
    fourier = images.shape[2]
    block_count = fourier // block_rows
    img_dev = images.shape[1]
    picks = orient.shape[2]
    levels = jnp.arange(block_count, dtype=jnp.int32)
    partial_value = jnp.einsum("jpr,rx->jpx", interp[0], volume, preferred_element_type=jnp.float32)
    owned_idx = lax.dynamic_slice_in_dim(block_index[0], slab_index * ori_dev, ori_dev, 0)
    received = lax.all_to_all(
        partial_value.reshape(slab_count, ori_dev * block_rows, 2 * fourier),
        "slab",
        split_axis=0,
        concat_axis=0,
        tiled=True,
    ).reshape(slab_count, ori_dev, block_rows, 2 * fourier)
    place = (owned_idx[:, :, None] == levels).astype(jnp.float32)
    summed = jnp.einsum(
        "osb,sopx->obpx",
        place,
        received,
        precision=lax.Precision.HIGHEST,
        preferred_element_type=jnp.float32,
    ).reshape(ori_dev, fourier, 2 * fourier)
    panels = lax.all_gather(summed.astype(jnp.bfloat16), "slab", axis=0, tiled=True)
    phase_fwd, phase_back = phase_tables(fourier, NS, BOX)
    blk = math.gcd(img_dev, 32)
    blk_total = img_dev // blk

    def per_block(pieces):
        image_blk, list_blk, defocus_blk = pieces
        return correlate(panels, image_blk, list_blk, defocus_blk, phase_fwd, phase_back, BOX)

    weights, backs = lax.map(
        per_block,
        (
            images[0].reshape(blk_total, blk, fourier, 2 * fourier),
            orient[0].reshape(blk_total, blk, picks),
            defocus[0].reshape(blk_total, blk),
        ),
    )
    all_slices = backs.reshape(img_dev * picks, 2 * fourier * fourier)
    member = (
        orient[0].reshape(-1)[:, None] == jnp.arange(orient_count, dtype=jnp.int32)[None, :]
    ).astype(jnp.bfloat16)
    contrib = lax.dot_general(
        member, all_slices, (((0,), (0,)), ((), ())), preferred_element_type=jnp.float32
    ).reshape(orient_count, fourier, 2 * fourier)
    back_own = lax.psum_scatter(contrib, "slab", scatter_dimension=0, tiled=True).astype(
        jnp.bfloat16
    )
    back_own = back_own.reshape(ori_dev, block_count, block_rows, 2 * fourier)
    chosen_back = (owned_idx[:, :, None] == levels).astype(jnp.bfloat16)
    outgoing = jnp.einsum(
        "osb,obpx->sopx", chosen_back, back_own, preferred_element_type=jnp.float32
    )
    outgoing = outgoing.astype(jnp.bfloat16).reshape(slab_count * ori_dev, block_rows, 2 * fourier)
    incoming = lax.all_to_all(outgoing, "slab", split_axis=0, concat_axis=0, tiled=True)
    column = jnp.einsum("jpr,jpx->rx", interp[0], incoming, preferred_element_type=jnp.float32)
    summed_cols = lax.psum(column, "img")
    update = summed_cols / math.sqrt(img_dev * slab_count)
    return (update, weights)


def solution(mesh):
    return jax.shard_map(
        on_device,
        mesh=mesh,
        in_specs=(
            P("slab", None),
            P("img", None, None, "slab"),
            P("img", None, None),
            P("img", "slab", None, None),
            P("img", "slab"),
            P("img", "slab", None),
        ),
        out_specs=(P("slab", None), P("img", "slab", None)),
        check_vma=False,
    )
```

profile of v0, /device:TPU:2, one launch (start us, length us, event | category | flops | bytes accessed | tf_op | source)
XLA Modules:
  0.0 444.3 jit_solution(18430927952869716344)
XLA Ops:
  8.4 2.4 fusion.10
  10.8 12.0 %all-to-all-start = ((f32[64,16,256]{2,1,0:T(8,128)}), f32[64,16,256]{2,1,0:T(8,128)S(1)}, u32[]{:S(2)}, u32[]{:S(2)}) async-start(f32[64,16,256]{2,1,0:T(8,128)} %fusion.10), calls=%async_computation | async-start | bytes 2097152 | tf_op jit(solution)/shard_map/all_to_all | solution.py:85
  23.5 26.4 %all-to-all-done = f32[64,16,256]{2,1,0:T(8,128)S(1)} async-done(((f32[64,16,256]{2,1,0:T(8,128)}), f32[64,16,256]{2,1,0:T(8,128)S(1)}, u32[]{:S(2)}, u32[]{:S(2)}) %all-to-all-start) | async-done | bytes 1048608 | tf_op jit(solution)/shard_map/all_to_all | solution.py:85
  54.4 5.4 %fusion.14 = (bf16[128,1,128,16]{2,3,1,0:T(8,128)(2,1)S(1)}, bf16[128,1,128,16]{2,3,1,0:T(8,128)(2,1)}, bf16[128,1,128,16]{2,3,1,0:T(8,128)(2,1)S(1)}) fusion(f32[128,16]{0,1:T(8,128)S(1)} %get-tuple-element.51, f32[128,16]{1,0:T(8,128)S(1)} %copy.68), kind=kLoop, calls=%fused_computation.32 | loop fusion | flops 1572864 | bytes 1589248 | tf_op jit(solution)/shard_map/convert.7
  62.6 2.6 convert_element_type.148
  65.5 3.9 add_negate_fusion
  71.7 56.5 %all-gather.2.cloned.1.call-done = bf16[64,128,256]{2,1,0:T(8,128)(2,1)} async-done(((bf16[1,128,256]{2,1,0:T(8,128)(2,1)}), bf16[64,128,256]{2,1,0:T(8,128)(2,1)}) %all-gather.2.cloned.1.call-update) | async-done | bytes 4194320 | tf_op jit(solution)/shard_map/all_gather | solution.py:100
  128.2 5.0 %gather_fusion = bf16[64,128,256]{2,1,0:T(8,128)(2,1)} fusion(bf16[64,128,256]{2,1,0:T(8,128)(2,1)} %all-gather.2.cloned.1.call-done, s32[1024]{0:T(1024)S(1)} %pad_clamp_fusion), kind=kCustom, calls=%fused_computation | custom fusion | bytes 8388864 | tf_op jit(solution)/shard_map/while/body/eval_jaxpr/gather | solution.py:49
  133.2 7.0 %copy.64 = f32[64,128,256]{1,2,0:T(8,128)} copy(bf16[64,128,256]{2,1,0:T(8,128)(2,1)} %gather_fusion) | data formatting | bytes 12582912 | tf_op jit(solution)/shard_map/while/body/eval_jaxpr/convert_element_type | solution.py:49
  140.2 7.8 %fusion.36 = (f32[16,4,128,1,128]{2,4,3,1,0:T(8,128)}, f32[16,4,128,1,128]{2,4,3,1,0:T(8,128)}) fusion(f32[16,4,128,2,128]{2,4,3,1,0:T(8,128)} %bitcast.62), kind=kLoop, calls=%fused_computation.73 | loop fusion | bytes 16777216 | tf_op jit(solution)/shard_map/while/body/eval_jaxpr/slice | solution.py:50
  148.0 5.5 %copy.84 = f32[16,4,128,1,128]{4,0,3,2,1:T(8,128)} copy(f32[16,4,128,1,128]{2,4,3,1,0:T(8,128)} %get-tuple-element.41) | data formatting | bytes 8388608
  153.4 5.5 %copy.85 = f32[16,4,128,1,128]{4,0,3,2,1:T(8,128)} copy(f32[16,4,128,1,128]{2,4,3,1,0:T(8,128)} %get-tuple-element.42) | data formatting | bytes 8388608
  158.9 4.9 %add_convert_fusion.1 = (bf16[16,4,128,1,128]{4,0,3,2,1:T(8,128)(2,1)S(1)}, bf16[16,4,128,1,128]{4,0,3,2,1:T(8,128)(2,1)S(1)}) fusion(f32[16,4,128,1,128]{4,0,3,2,1:T(8,128)} %copy.85, f32[16,4,128,1,128]{4,0,3,2,1:T(8,128)} %copy.84, f32[16,128,128]{2,0,1:T(8,128)} %get-tuple-element.44, f32[16,128,128]{2,0,1:T(8,128)S(1)} %get-tuple-element.43), kind=kLoop, calls=%fused_computation.9 | loop fusion | flops 8388608 | bytes 14680064 | tf_op jit(solution)/shard_map/convert.8
  164.2 6.6 %copy.67 = bf16[16,4,128,2,128]{4,3,2,1,0:T(2,128)(2,1)} copy(bf16[16,4,128,2,128]{4,0,3,2,1:T(8,128)(2,1)S(1)} %pad_maximum_fusion) | data formatting | bytes 8388608 | tf_op jit(solution)/shard_map/while/body/eval_jaxpr/stack | solution.py:52
  170.8 7.8 %convert_element_type.145 = bf16[64,32768]{1,0:T(8,128)(2,1)} reshape(bf16[16,4,128,2,128]{4,3,2,1,0:T(2,128)(2,1)} %copy.67) | data formatting | bytes 8388608 | tf_op jit(solution)/shard_map/while/body/eval_jaxpr/convert_element_type | solution.py:55
  178.6 3.7 fusion.37
  182.9 2.4 fusion.6
  187.1 6.6 %copy.72 = bf16[16,4,128,2,128]{4,3,2,1,0:T(2,128)(2,1)} copy(bf16[16,4,128,2,128]{4,0,3,2,1:T(8,128)(2,1)S(1)} %pad_maximum_fusion.1) | data formatting | bytes 8388608 | tf_op jit(solution)/shard_map/while/body/eval_jaxpr/stack | solution.py:65
  193.7 7.8 %convert_element_type.150 = bf16[64,32768]{1,0:T(8,128)(2,1)} reshape(bf16[16,4,128,2,128]{4,3,2,1,0:T(2,128)(2,1)} %copy.72) | data formatting | bytes 8388608 | tf_op jit(solution)/shard_map/while/body/eval_jaxpr/convert_element_type | solution.py:68
  201.5 3.4 fusion
  205.0 8.1 %copy.74 = f32[64,128,256]{2,1,0:T(8,128)} copy(f32[64,128,256]{2,0,1:T(8,128)S(1)} %fusion) | data formatting | bytes 16777216 | tf_op jit(solution)/shard_map/dot_general | solution.py:121
  213.1 149.0 %reduce-scatter.2.cloned.1.call-done = f32[1,128,256]{2,1,0:T(8,128)} async-done(((f32[64,128,256]{2,1,0:T(8,128)}), f32[1,128,256]{2,1,0:T(8,128)}) %reduce-scatter.2.cloned.1.call-update) | async-done | bytes 131088 | tf_op jit(solution)/shard_map/reduce_scatter | solution.py:124
  363.7 24.8 %all_to_all.10 = bf16[64,16,256]{2,1,0:T(8,128)(2,1)S(1)} all-to-all(bf16[64,16,256]{2,1,0:T(8,128)(2,1)S(1)} %copy.76), channel_id=1, replica_groups=mesh['slab'=64,'img'=4] {'slab'}, dimensions={0} | all-to-all | bytes 1048576 | tf_op jit(solution)/shard_map/all_to_all | solution.py:133
  390.6 45.1 %all-reduce.2.cloned.1.call-done = f32[512,256]{0,1:T(8,128)} async-done(((f32[512,256]{0,1:T(8,128)}), f32[512,256]{0,1:T(8,128)}) %all-reduce.2.cloned.1.call-update) | async-done | bytes 524304 | tf_op jit(solution)/shard_map/psum | solution.py:135
  (58 shorter events, 20.3 us)
Async XLA Ops:
  7.2 1.2 copy-start
  7.2 44.7 %copy-start.4 = (s32[1,16,4]{1,2,0:T(4,128)S(1)}, s32[1,16,4]{1,2,0:T(4,128)}, u32[]{:S(2)}) copy-start(s32[1,16,4]{1,2,0:T(4,128)} %param.11) | copy-start | bytes 772
  10.8 39.2 %all-to-all-start = ((f32[64,16,256]{2,1,0:T(8,128)}), f32[64,16,256]{2,1,0:T(8,128)S(1)}, u32[]{:S(2)}, u32[]{:S(2)}) async-start(f32[64,16,256]{2,1,0:T(8,128)} %fusion.10), calls=%async_computation | async-start | bytes 2097152 | tf_op jit(solution)/shard_map/all_to_all | solution.py:85
  22.8 105.4 %all-gather.2.cloned.1.call-start = ((), (), s32[]{:S(2)}) async-start(), calls=%async_computation.3 | async-start | bytes 4259840 | tf_op jit(solution)/shard_map/all_gather | solution.py:100
  51.6 310.5 %reduce-scatter.2.cloned.1.call-start = ((), (), s32[]{:S(2)}) async-start(), calls=%async_computation.4 | async-start | bytes 8519680 | tf_op jit(solution)/shard_map/reduce_scatter | solution.py:124
  54.2 11.1 %copy-start.5 = (f32[1,16]{1,0:T(1,128)S(1)}, f32[1,16]{1,0:T(1,128)}, u32[]{:S(2)}) copy-start(f32[1,16]{1,0:T(1,128)} %param.10) | copy-start | bytes 196
  59.8 0.8 copy-start.2
  178.6 4.3 copy-start.3
  182.9 2.4 copy-start.1
  213.1 222.6 %all-reduce.2.cloned.1.call-start = ((), (), s32[]{:S(2)}) async-start(), calls=%async_computation.5 | async-start | bytes 1048576 | tf_op jit(solution)/shard_map/psum | solution.py:135
Sparse Core Ops, SparseCore 0:
  51.7 76.3 all-gather.1
  213.2 148.8 reduce-scatter.1
  389.9 45.7 all-reduce.1
where the time goes:
time: 445 us; the launch traced here: 444 us
  waiting for transfers between devices  277 us (62%)
  local copies, waits for them, and re-layouts  80.9 us (18%)
  blocking collectives  24.8 us (6%)
  other arithmetic  20.7 us (5%)
  matrix products  14.5 us (3%)
  between operations  14 us (3%)
  starting transfers between devices  12.3 us (3%)
    reduce_scatter x1, waiting for transfers between devices, on_device(): lax.psum_scatter(contrib, 'slab', scatter_dimension=0, tiled=True)  149 us
    all_gather x1, waiting for transfers between devices, on_device(): lax.all_gather(summed.astype(jnp.bfloat16), 'slab', axis=0, tiled=True)  56.5 us
    psum x1, waiting for transfers between devices, on_device(): summed_cols = lax.psum(column, 'img')  45.1 us
    all_to_all x1, waiting for transfers between devices, on_device(): lax.all_to_all(partial_value.reshape(slab_count, ori_dev * block_rows, 2...  26.4 us
    all_to_all x1, blocking collectives, on_device(): lax.all_to_all(outgoing, 'slab', split_axis=0, concat_axis=0, tiled=True)  24.8 us
    unnamed x16, local copies, waits for them, and re-layouts  14.1 us
    all_to_all x1, starting transfers between devices, on_device(): lax.all_to_all(partial_value.reshape(slab_count, ori_dev * block_rows, 2...  12 us
    another operation x3, other arithmetic  11.8 us
  transfers between devices with their start and end apart: 4, of which 4 were waited for; matrix products, arithmetic and copies ran while one was open for 5% of the time, Pallas kernels for 0%

commit v1 on v0

--- a/solution.py
+++ b/solution.py
@@ -10,6 +10,14 @@
 aberration = 27000000.0
 amplitude = 0.1
 grid_side = 4
+
+
+def doubling_sum(x, axis):
+    peers, total = (lax.axis_size(axis), x)
+    for far in [1 << k for k in range(peers.bit_length() - 1)]:
+        pairs = [(i, i ^ far) for i in range(peers)]
+        total = total + lax.ppermute(total, axis, pairs)
+    return total
 
 
 def phase_tables(fourier, shifts, box):
@@ -132,7 +140,7 @@
     outgoing = outgoing.astype(jnp.bfloat16).reshape(slab_count * ori_dev, block_rows, 2 * fourier)
     incoming = lax.all_to_all(outgoing, "slab", split_axis=0, concat_axis=0, tiled=True)
     column = jnp.einsum("jpr,jpx->rx", interp[0], incoming, preferred_element_type=jnp.float32)
-    summed_cols = lax.psum(column, "img")
+    summed_cols = doubling_sum(column, "img")
     update = summed_cols / math.sqrt(img_dev * slab_count)
     return (update, weights)
 

time: 445 us -> 428 us (0.962)
  waiting for transfers between devices: 277 us -> 256 us
  starting transfers between devices: 12.3 us -> 17 us
    psum x1 -> x0, waiting for transfers between devices: 45.1 us -> none  [on_device(): summed_cols = lax.psum(column, 'img')]
    ppermute x0 -> x2, waiting for transfers between devices: none -> 24.3 us  [doubling_sum(): total = total + lax.ppermute(total, axis, pairs)]
    ppermute x0 -> x2, starting transfers between devices: none -> 4.67 us  [doubling_sum(): total = total + lax.ppermute(total, axis, pairs)]
  transfers between devices with their start and end apart: 4 -> 5, of which waited for: 4 -> 5; matrix products, arithmetic and copies ran while one was open for 5% -> 5% of each run, Pallas kernels for 0% -> 0%
where the time goes in v1:
time: 428 us; the launch traced here: 427 us
  waiting for transfers between devices  256 us (60%)
  local copies, waits for them, and re-layouts  81.1 us (19%)
  blocking collectives  24.8 us (6%)
  other arithmetic  19.8 us (5%)
  starting transfers between devices  17 us (4%)
  between operations  14.3 us (3%)
  matrix products  13.7 us (3%)
    reduce_scatter x1, waiting for transfers between devices, on_device(): lax.psum_scatter(contrib, 'slab', scatter_dimension=0, tiled=True)  149 us
    all_gather x1, waiting for transfers between devices, on_device(): lax.all_gather(summed.astype(jnp.bfloat16), 'slab', axis=0, tiled=True)  56.5 us
    all_to_all x1, waiting for transfers between devices, on_device(): lax.all_to_all(partial_value.reshape(slab_count, ori_dev * block_rows, 2...  26.4 us
    all_to_all x1, blocking collectives, on_device(): lax.all_to_all(outgoing, 'slab', split_axis=0, concat_axis=0, tiled=True)  24.8 us
    ppermute x2, waiting for transfers between devices, doubling_sum(): total = total + lax.ppermute(total, axis, pairs)  24.3 us
    unnamed x16, local copies, waits for them, and re-layouts  14.1 us
    all_to_all x1, starting transfers between devices, on_device(): lax.all_to_all(partial_value.reshape(slab_count, ori_dev * block_rows, 2...  12 us
    another operation x3, other arithmetic  11.8 us
  transfers between devices with their start and end apart: 5, of which 5 were waited for; matrix products, arithmetic and copies ran while one was open for 5% of the time, Pallas kernels for 0%

profile of v1, /device:TPU:2, one launch (start us, length us, event | category | flops | bytes accessed | tf_op | source)
XLA Modules:
  0.0 426.8 jit_solution(9064254444183800111)
XLA Ops:
  10.8 12.0 %all-to-all-start = ((f32[64,16,256]{2,1,0:T(8,128)}), f32[64,16,256]{2,1,0:T(8,128)S(1)}, u32[]{:S(2)}, u32[]{:S(2)}) async-start(f32[64,16,256]{2,1,0:T(8,128)} %fusion.10), calls=%async_computation | async-start | bytes 2097152 | tf_op jit(solution)/shard_map/all_to_all | solution.py:93
  23.5 26.4 %all-to-all-done = f32[64,16,256]{2,1,0:T(8,128)S(1)} async-done(((f32[64,16,256]{2,1,0:T(8,128)}), f32[64,16,256]{2,1,0:T(8,128)S(1)}, u32[]{:S(2)}, u32[]{:S(2)}) %all-to-all-start) | async-done | bytes 1048608 | tf_op jit(solution)/shard_map/all_to_all | solution.py:93
  54.4 5.4 %fusion.14 = (bf16[128,1,128,16]{2,3,1,0:T(8,128)(2,1)S(1)}, bf16[128,1,128,16]{2,3,1,0:T(8,128)(2,1)}, bf16[128,1,128,16]{2,3,1,0:T(8,128)(2,1)S(1)}) fusion(f32[128,16]{0,1:T(8,128)S(1)} %get-tuple-element.51, f32[128,16]{1,0:T(8,128)S(1)} %copy.68), kind=kLoop, calls=%fused_computation.32 | loop fusion | flops 1572864 | bytes 1589248 | tf_op jit(solution)/shard_map/convert.7
  62.6 2.6 convert_element_type.148
  65.5 3.9 add_negate_fusion
  71.7 56.5 %all-gather.2.cloned.1.call-done = bf16[64,128,256]{2,1,0:T(8,128)(2,1)} async-done(((bf16[1,128,256]{2,1,0:T(8,128)(2,1)}), bf16[64,128,256]{2,1,0:T(8,128)(2,1)}) %all-gather.2.cloned.1.call-update) | async-done | bytes 4194320 | tf_op jit(solution)/shard_map/all_gather | solution.py:108
  128.2 5.0 %gather_fusion = bf16[64,128,256]{2,1,0:T(8,128)(2,1)} fusion(bf16[64,128,256]{2,1,0:T(8,128)(2,1)} %all-gather.2.cloned.1.call-done, s32[1024]{0:T(1024)S(1)} %pad_clamp_fusion), kind=kCustom, calls=%fused_computation | custom fusion | bytes 8388864 | tf_op jit(solution)/shard_map/while/body/eval_jaxpr/gather | solution.py:57
  133.2 7.0 %copy.64 = f32[64,128,256]{1,2,0:T(8,128)} copy(bf16[64,128,256]{2,1,0:T(8,128)(2,1)} %gather_fusion) | data formatting | bytes 12582912 | tf_op jit(solution)/shard_map/while/body/eval_jaxpr/convert_element_type | solution.py:57
  140.2 7.8 %fusion.36 = (f32[16,4,128,1,128]{2,4,3,1,0:T(8,128)}, f32[16,4,128,1,128]{2,4,3,1,0:T(8,128)}) fusion(f32[16,4,128,2,128]{2,4,3,1,0:T(8,128)} %bitcast.62), kind=kLoop, calls=%fused_computation.73 | loop fusion | bytes 16777216 | tf_op jit(solution)/shard_map/while/body/eval_jaxpr/slice | solution.py:58
  148.0 5.5 %copy.84 = f32[16,4,128,1,128]{4,0,3,2,1:T(8,128)} copy(f32[16,4,128,1,128]{2,4,3,1,0:T(8,128)} %get-tuple-element.41) | data formatting | bytes 8388608
  153.5 5.5 %copy.85 = f32[16,4,128,1,128]{4,0,3,2,1:T(8,128)} copy(f32[16,4,128,1,128]{2,4,3,1,0:T(8,128)} %get-tuple-element.42) | data formatting | bytes 8388608
  159.0 4.9 %add_convert_fusion.1 = (bf16[16,4,128,1,128]{4,0,3,2,1:T(8,128)(2,1)S(1)}, bf16[16,4,128,1,128]{4,0,3,2,1:T(8,128)(2,1)S(1)}) fusion(f32[16,4,128,1,128]{4,0,3,2,1:T(8,128)} %copy.85, f32[16,4,128,1,128]{4,0,3,2,1:T(8,128)} %copy.84, f32[16,128,128]{2,0,1:T(8,128)} %get-tuple-element.44, f32[16,128,128]{2,0,1:T(8,128)S(1)} %get-tuple-element.43), kind=kLoop, calls=%fused_computation.9 | loop fusion | flops 8388608 | bytes 14680064 | tf_op jit(solution)/shard_map/convert.8
  164.3 6.6 %copy.67 = bf16[16,4,128,2,128]{4,3,2,1,0:T(2,128)(2,1)} copy(bf16[16,4,128,2,128]{4,0,3,2,1:T(8,128)(2,1)S(1)} %pad_maximum_fusion) | data formatting | bytes 8388608 | tf_op jit(solution)/shard_map/while/body/eval_jaxpr/stack | solution.py:60
  170.9 7.8 %convert_element_type.145 = bf16[64,32768]{1,0:T(8,128)(2,1)} reshape(bf16[16,4,128,2,128]{4,3,2,1,0:T(2,128)(2,1)} %copy.67) | data formatting | bytes 8388608 | tf_op jit(solution)/shard_map/while/body/eval_jaxpr/convert_element_type | solution.py:63
  178.7 3.7 fusion.37
  187.2 6.6 %copy.72 = bf16[16,4,128,2,128]{4,3,2,1,0:T(2,128)(2,1)} copy(bf16[16,4,128,2,128]{4,0,3,2,1:T(8,128)(2,1)S(1)} %pad_maximum_fusion.1) | data formatting | bytes 8388608 | tf_op jit(solution)/shard_map/while/body/eval_jaxpr/stack | solution.py:73
  193.8 7.9 %convert_element_type.150 = bf16[64,32768]{1,0:T(8,128)(2,1)} reshape(bf16[16,4,128,2,128]{4,3,2,1,0:T(2,128)(2,1)} %copy.72) | data formatting | bytes 8388608 | tf_op jit(solution)/shard_map/while/body/eval_jaxpr/convert_element_type | solution.py:76
  201.7 3.4 fusion
  205.1 8.1 %copy.74 = f32[64,128,256]{2,1,0:T(8,128)} copy(f32[64,128,256]{2,0,1:T(8,128)S(1)} %fusion) | data formatting | bytes 16777216 | tf_op jit(solution)/shard_map/dot_general | solution.py:129
  213.2 149.0 %reduce-scatter.2.cloned.1.call-done = f32[1,128,256]{2,1,0:T(8,128)} async-done(((f32[64,128,256]{2,1,0:T(8,128)}), f32[1,128,256]{2,1,0:T(8,128)}) %reduce-scatter.2.cloned.1.call-update) | async-done | bytes 131088 | tf_op jit(solution)/shard_map/reduce_scatter | solution.py:132
  363.7 24.8 %all_to_all.10 = bf16[64,16,256]{2,1,0:T(8,128)(2,1)S(1)} all-to-all(bf16[64,16,256]{2,1,0:T(8,128)(2,1)S(1)} %copy.76), channel_id=1, replica_groups=mesh['slab'=64,'img'=4] {'slab'}, dimensions={0} | all-to-all | bytes 1048576 | tf_op jit(solution)/shard_map/all_to_all | solution.py:141
  390.6 13.0 %collective-permute-done = f32[512,256]{0,1:T(8,128)S(1)} collective-permute-done((f32[512,256]{0,1:T(8,128)S(1)}, f32[512,256]{0,1:T(8,128)S(1)}, u32[]{:S(2)}, u32[]{:S(2)}) %collective-permute-start) | collective-permute-done | bytes 524320 | tf_op jit(solution)/shard_map/ppermute | solution.py:19
  403.6 3.1 collective-permute-start.1
  407.6 11.3 %collective-permute-done.1 = f32[512,256]{0,1:T(8,128)S(1)} collective-permute-done((f32[512,256]{0,1:T(8,128)S(1)}, f32[512,256]{0,1:T(8,128)S(1)}, u32[]{:S(2)}, u32[]{:S(2)}) %collective-permute-start.1) | collective-permute-done | bytes 524320 | tf_op jit(solution)/shard_map/ppermute | solution.py:19
  (60 shorter events, 24.8 us)
Async XLA Ops:
  7.2 1.2 copy-start
  7.2 44.7 %copy-start.4 = (s32[1,16,4]{1,2,0:T(4,128)S(1)}, s32[1,16,4]{1,2,0:T(4,128)}, u32[]{:S(2)}) copy-start(s32[1,16,4]{1,2,0:T(4,128)} %param.11) | copy-start | bytes 772
  10.8 39.2 %all-to-all-start = ((f32[64,16,256]{2,1,0:T(8,128)}), f32[64,16,256]{2,1,0:T(8,128)S(1)}, u32[]{:S(2)}, u32[]{:S(2)}) async-start(f32[64,16,256]{2,1,0:T(8,128)} %fusion.10), calls=%async_computation | async-start | bytes 2097152 | tf_op jit(solution)/shard_map/all_to_all | solution.py:93
  22.8 105.4 %all-gather.2.cloned.1.call-start = ((), (), s32[]{:S(2)}) async-start(), calls=%async_computation.3 | async-start | bytes 4259840 | tf_op jit(solution)/shard_map/all_gather | solution.py:108
  51.6 310.6 %reduce-scatter.2.cloned.1.call-start = ((), (), s32[]{:S(2)}) async-start(), calls=%async_computation.4 | async-start | bytes 8519680 | tf_op jit(solution)/shard_map/reduce_scatter | solution.py:132
  54.2 11.2 %copy-start.5 = (f32[1,16]{1,0:T(1,128)S(1)}, f32[1,16]{1,0:T(1,128)}, u32[]{:S(2)}) copy-start(f32[1,16]{1,0:T(1,128)} %param.10) | copy-start | bytes 196
  59.8 0.8 copy-start.2
  178.7 4.3 copy-start.3
  183.0 2.4 copy-start.1
  389.0 14.5 %collective-permute-start = (f32[512,256]{0,1:T(8,128)S(1)}, f32[512,256]{0,1:T(8,128)S(1)}, u32[]{:S(2)}, u32[]{:S(2)}) collective-permute-start(f32[512,256]{0,1:T(8,128)S(1)} %convolution_bitcast_fusion), channel_id=1, source_target_pairs={{0,1},{1,0},{2,3},{3,2},{4,5},{5,4},{6,7},{7,6},{8,9},{9,8},{10,11... | collective-permute-start | bytes 1572872 | tf_op jit(solution)/shard_map/ppermute | solution.py:19
  403.6 15.3 %collective-permute-start.1 = (f32[512,256]{0,1:T(8,128)S(1)}, f32[512,256]{0,1:T(8,128)S(1)}, u32[]{:S(2)}, u32[]{:S(2)}) collective-permute-start(f32[512,256]{0,1:T(8,128)S(1)} %add.191), channel_id=1, source_target_pairs={{0,2},{1,3},{2,0},{3,1},{4,6},{5,7},{6,4},{7,5},{8,10},{9,11},{10,... | collective-permute-start | bytes 1572872 | tf_op jit(solution)/shard_map/ppermute | solution.py:19
Sparse Core Ops, SparseCore 0:
  51.7 76.3 all-gather.1
  213.3 148.7 reduce-scatter.1
